TPU v7x, 512 devices: a whole 4x8x8 slice. The times are simulated.
512 devices in a mesh: row: 64 (over y, z), col: 8 (over x, core).
Axes of the slice: x: 4, y: 8, z: 8, core: 2. Of those that a mesh axis runs over, the one named last changes fastest.
Arguments:
- object_field: float32 [2, 16384, 2048], P(None, 'row', 'col'), may hold values from -6 to 6
- probe_field: float32 [2, 256, 256], replicated, may hold values from -6 to 6
- amplitudes: float32 [128, 2048, 256], P('row', 'col'), may hold values from 0 to 4
- offsets: int32 [64, 8, 2, 2], P('row', 'col'), may hold values from 0 to 128, as said below
- counts: int32 [64, 8], P('row', 'col'), may hold values from 1 to 2
Outputs:
- object_out: float32 [2, 16384, 2048], P(None, 'row', 'col')
- probe_out: float32 [2, 256, 256], replicated
Inputs may be any that keep to these rules, and one draw needn't show every extreme that they name: `offsets`: slots from counts[r, c] on are padding and hold no window.
All inputs are finite; a program needn't handle non-finite values.
Results may differ from a plain program's by a relative error of at most 0.0003.
Values sent between devices are 32-bit elements; how exact they have to be, the bound alone decides.
No kernel may reach another device: no remote copies, remote signals or barrier semaphores. Data moves between devices by JAX's collectives and lax.ppermute only.
A program may use at most 64 MiB of HBM per device.

v0:
```python
import math
import jax
import jax.numpy as jnp
from jax import lax
from jax.sharding import PartitionSpec as P

HALO = 128
OUTER = 2
smooth_floor = 0.5
object_step = 0.5
tiny_value = 1e-06


def shifted(value, axis, by):
    length = lax.axis_size(axis)
    pairs = [(i, i + by) for i in range(length) if 0 <= i + by < length]
    return lax.ppermute(value, axis, pairs)


def make_tables(length):
    indices = jnp.arange(length, dtype=jnp.int32)
    product = indices[:, None] * indices[None, :] % length
    angles = product.astype(jnp.float32) * (2.0 * math.pi / length)
    norming = 1.0 / math.sqrt(length)
    cosine_table = jnp.cos(angles) * norming
    sine_table = jnp.sin(angles) * norming
    forward = (cosine_table, -sine_table - cosine_table, cosine_table - sine_table)
    inverse = (cosine_table, sine_table - cosine_table, cosine_table + sine_table)
    return (forward, inverse)


def complex_product(real_part, imag_part, matrices, pattern):
    first_term = jnp.einsum(
        pattern, real_part + imag_part, matrices[0], precision=lax.Precision.HIGHEST
    )
    second_term = jnp.einsum(pattern, real_part, matrices[1], precision=lax.Precision.HIGHEST)
    third_term = jnp.einsum(pattern, imag_part, matrices[2], precision=lax.Precision.HIGHEST)
    return (first_term - third_term, first_term + second_term)


def transform(real_part, imag_part, matrices):
    rows_real, rows_imag = complex_product(real_part, imag_part, matrices, "bjk,kw->bjw")
    return complex_product(rows_real, rows_imag, matrices, "bkw,jk->bjw")


def window_terms(win_real, win_imag, measured, probe_real, probe_imag, forward, inverse):
    psi_real = probe_real * win_real - probe_imag * win_imag
    psi_imag = probe_real * win_imag + probe_imag * win_real
    hat_real, hat_imag = transform(psi_real, psi_imag, forward)
    ratio_term = measured / jnp.sqrt(hat_real * hat_real + hat_imag * hat_imag + smooth_floor) - 1.0
    return transform(hat_real * ratio_term, hat_imag * ratio_term, inverse)


def add_window(grid_now, terms, first_row, first_col):
    zero_index = jnp.zeros((), jnp.int32)
    present = lax.dynamic_slice(grid_now, (zero_index, first_row, first_col), terms.shape)
    return lax.dynamic_update_slice(grid_now, present + terms, (zero_index, first_row, first_col))


def shards(object_field, probe_field, amplitudes, offsets, counts):
    tile_rows = object_field.shape[1]
    tile_cols = object_field.shape[2]
    window = probe_field.shape[1]
    slot_count = amplitudes.shape[0]
    margin = HALO
    forward, inverse = make_tables(window)
    count_here = counts[0, 0]
    current = object_field
    probe_now = probe_field
    for outer_step in range(OUTER):
        probe_real = probe_now[0]
        probe_imag = probe_now[1]
        probe_mean = jnp.sum(probe_now * probe_now) / (window * window)
        lower_rows = shifted(current[:, :margin, :], "row", -1)
        taller = jnp.concatenate([current, lower_rows], axis=1)
        right_cols = shifted(taller[:, :, :margin], "col", -1)
        extended = jnp.concatenate([taller, right_cols], axis=2)
        grad_ext = jnp.zeros_like(extended)
        zero_index = jnp.zeros((), jnp.int32)
        window_list = [
            lax.dynamic_slice(
                extended,
                (zero_index, offsets[0, 0, slot_index, 0], offsets[0, 0, slot_index, 1]),
                (2, window, window),
            )
            for slot_index in range(slot_count)
        ]
        stacked = jnp.stack(window_list, axis=1)
        win_real = stacked[0]
        win_imag = stacked[1]
        diff_real, diff_imag = window_terms(
            win_real, win_imag, amplitudes, probe_real, probe_imag, forward, inverse
        )
        live_mask = (jnp.arange(slot_count, dtype=jnp.int32) < count_here).astype(jnp.float32)[
            :, None, None
        ]
        diff_real = diff_real * live_mask
        diff_imag = diff_imag * live_mask
        object_real = probe_real * diff_real + probe_imag * diff_imag
        object_imag = probe_real * diff_imag - probe_imag * diff_real
        probe_grad = jnp.stack(
            [
                jnp.sum(win_real * diff_real + win_imag * diff_imag, axis=0),
                jnp.sum(win_real * diff_imag - win_imag * diff_real, axis=0),
            ]
        )
        power_sum = jnp.sum(live_mask * (win_real * win_real + win_imag * win_imag))
        for slot_index in range(slot_count):
            terms = jnp.stack([object_real[slot_index], object_imag[slot_index]])
            grad_ext = add_window(
                grad_ext, terms, offsets[0, 0, slot_index, 0], offsets[0, 0, slot_index, 1]
            )
        rim_right = shifted(grad_ext[:, :, tile_cols:], "col", 1)
        narrowed = grad_ext[:, :, :tile_cols]
        narrowed = jnp.concatenate(
            [narrowed[:, :, :margin] + rim_right, narrowed[:, :, margin:]], axis=2
        )
        rim_lower = shifted(narrowed[:, tile_rows:, :], "row", 1)
        tile_grad = jnp.concatenate(
            [narrowed[:, :margin, :] + rim_lower, narrowed[:, margin:tile_rows, :]], axis=1
        )
        current = current + object_step * tile_grad / (probe_mean + tiny_value)
        power_old = jnp.sum(probe_now * probe_now)
        summed_grad, summed_power = lax.psum((probe_grad, power_sum), ("row", "col"))
        moved_probe = probe_now + summed_grad / (summed_power / (window * window) + tiny_value)
        power_new = jnp.sum(moved_probe * moved_probe)
        probe_now = moved_probe * jnp.sqrt(power_old / (power_new + tiny_value))
    return (current, probe_now)


def solution(mesh):
    return jax.shard_map(
        shards,
        mesh=mesh,
        in_specs=(
            P(None, "row", "col"),
            P(),
            P("row", "col", None),
            P("row", "col", None, None),
            P("row", "col"),
        ),
        out_specs=(P(None, "row", "col"), P()),
        check_vma=False,
    )
```

profile of v0, /device:TPU:21, one launch (start us, length us, event | category | flops | bytes accessed | tf_op | source)
XLA Modules:
  0.0 694.5 jit_solution(13178830681612049637)
XLA Ops:
  8.2 10.7 %collective-permute-start = (f32[2,128,256]{2,1,0:T(8,128)S(1)}, f32[2,128,256]{2,1,0:T(8,128)S(1)}, u32[]{:S(2)}, u32[]{:S(2)}) collective-permute-start(f32[2,128,256]{2,1,0:T(8,128)S(1)} %slice.127), channel_id=1, source_target_pairs={{8,0},{16,8},{24,16},{32,24},{40,32},{48,40},{56,48},{64,56},{72,6... | collective-permute-start | bytes 786440 | tf_op jit(solution)/shard_map/ppermute | solution.py:17
  20.0 3.9 collective-permute-done
  23.9 3.4 collective-permute-start.1
  37.1 1.6 fusion.48
  38.8 1.7 convolution_add_fusion.7
  40.5 1.7 convolution_subtract_fusion.7
  42.2 1.7 fusion.46
  43.8 1.7 fusion.10
  45.6 1.7 fusion.11
  47.3 2.0 fusion.42
  49.3 1.8 convolution_add_fusion.5
  51.1 1.8 convolution_subtract_fusion.5
  52.9 1.7 fusion.40
  54.5 1.7 fusion.9
  56.3 2.4 add_reduce_fusion.1
  59.6 7.6 %dynamic_update_slice.12 = f32[2,384,384]{2,1,0:T(8,128)S(1)} dynamic-update-slice(f32[2,384,384]{2,1,0:T(8,128)S(1)} %broadcast.28.clone, f32[2,256,256]{2,1,0:T(8,128)S(1)} %pad_maximum_fusion.3, s32[]{:T(128)} %constant.29.clone.1, s32[]{:T(128)S(6)} %select_n.82, s32[]{:T(128)S(6)} %select_n.83) | dynamic-update-slice | bytes 1048580 | tf_op jit(solution)/shard_map/dynamic_update_slice | solution.py:57
  67.2 1.2 maximum_add_fusion
  68.4 7.0 %dynamic_update_slice.13 = f32[2,384,384]{2,1,0:T(8,128)S(1)} dynamic-update-slice(f32[2,384,384]{2,1,0:T(8,128)S(1)} %dynamic_update_slice.12, f32[2,256,256]{2,1,0:T(8,128)S(1)} %maximum_add_fusion, s32[]{:T(128)} %constant.29.clone.1, s32[]{:T(128)S(6)} %select_n.84, s32[]{:T(128)S(6)} %select_n.85) | dynamic-update-slice | bytes 1048580 | tf_op jit(solution)/shard_map/dynamic_update_slice | solution.py:57
  75.4 2.8 collective-permute-start.2
  79.1 3.8 collective-permute-done.2
  84.0 1.9 collective-permute-start.3
  86.0 101.0 %psum.29 = f32[]{:T(128)} all-reduce(f32[]{:T(128)} %get-tuple-element.7), channel_id=1, replica_groups=mesh['row'=64,'col'=8] {'row','col'}, use_global_device_ids=true, to_apply=%region_5.6 | all-reduce | flops 1 | bytes 8 | tf_op jit(solution)/shard_map/psum | solution.py:124
  187.6 165.8 %all-reduce.3.cloned.1.call-done = f32[2,256,256]{2,1,0:T(8,128)} async-done(((f32[2,256,256]{2,1,0:T(8,128)}), f32[2,256,256]{2,1,0:T(8,128)}) %all-reduce.3.cloned.1.call-update) | async-done | bytes 524304 | tf_op jit(solution)/shard_map/psum | solution.py:124
  353.4 1.8 multiply_reduce_fusion.3
  356.0 2.1 collective-permute-start.4
  359.4 6.7 collective-permute-done.4
  366.1 2.5 collective-permute-start.5
  368.8 6.5 collective-permute-done.5
  375.8 1.6 fusion.38
  377.4 1.7 convolution_add_fusion.3
  379.1 1.7 convolution_subtract_fusion.3
  380.8 1.7 fusion.36
  382.4 1.7 fusion.4
  384.2 1.7 fusion.5
  385.9 1.9 fusion.32
  387.8 1.8 convolution_add_fusion.1
  389.6 1.8 convolution_subtract_fusion.1
  391.3 1.7 fusion.30
  393.0 1.7 fusion.3
  394.7 2.4 add_reduce_fusion
  398.2 7.6 %dynamic_update_slice.14 = f32[2,384,384]{2,1,0:T(8,128)S(1)} dynamic-update-slice(f32[2,384,384]{2,1,0:T(8,128)S(1)} %broadcast.28, f32[2,256,256]{2,1,0:T(8,128)S(1)} %pad_maximum_fusion.5, s32[]{:T(128)} %constant.29.clone.1, s32[]{:T(128)S(6)} %select_n.82, s32[]{:T(128)S(6)} %select_n.83) | dynamic-update-slice | bytes 1048580 | tf_op jit(solution)/shard_map/dynamic_update_slice | solution.py:57
  406.0 7.0 %dynamic_update_slice.15 = f32[2,384,384]{2,1,0:T(8,128)S(1)} dynamic-update-slice(f32[2,384,384]{2,1,0:T(8,128)S(1)} %dynamic_update_slice.14, f32[2,256,256]{2,1,0:T(8,128)S(1)} %maximum_add_fusion.1, s32[]{:T(128)} %constant.29.clone.1, s32[]{:T(128)S(6)} %select_n.84, s32[]{:T(128)S(6)} %select_n.85) | dynamic-update-slice | bytes 1048580 | tf_op jit(solution)/shard_map/dynamic_update_slice | solution.py:57
  413.1 1.9 collective-permute-start.6
  415.0 98.3 %psum.31 = f32[]{:T(128)} all-reduce(f32[]{:T(128)} %get-tuple-element.6), channel_id=1, replica_groups=mesh['row'=64,'col'=8] {'row','col'}, use_global_device_ids=true, to_apply=%region_12.13 | all-reduce | flops 1 | bytes 8 | tf_op jit(solution)/shard_map/psum | solution.py:124
  514.0 155.3 %all-reduce.5.cloned.1.call-done = f32[2,256,256]{2,1,0:T(8,128)} async-done(((f32[2,256,256]{2,1,0:T(8,128)}), f32[2,256,256]{2,1,0:T(8,128)}) %all-reduce.5.cloned.1.call-update) | async-done | bytes 524304 | tf_op jit(solution)/shard_map/psum | solution.py:124
  669.3 1.8 multiply_reduce_fusion
  674.3 1.9 collective-permute-start.7
  677.1 9.3 %collective-permute-done.7 = f32[2,128,256]{2,1,0:T(8,128)S(1)} collective-permute-done((f32[2,128,256]{2,1,0:T(8,128)S(1)}, f32[2,128,256]{2,1,0:T(8,128)S(1)}, u32[]{:S(2)}, u32[]{:S(2)}) %collective-permute-start.7) | collective-permute-done | bytes 262176 | tf_op jit(solution)/shard_map/ppermute | solution.py:17
  (56 shorter events, 11.5 us)
Async XLA Ops:
  7.2 346.2 %all-reduce.3.cloned.1.call-start = ((), (), s32[]{:S(2)}) async-start(), calls=%async_computation | async-start | bytes 1048576 | tf_op jit(solution)/shard_map/psum | solution.py:124
  8.2 19.2 %copy-start.5 = (s32[1,1,2,2]{3,2,1,0:T(2,128)S(1)}, s32[1,1,2,2]{3,2,1,0:T(2,128)}, u32[]{:S(2)}) copy-start(s32[1,1,2,2]{3,2,1,0:T(2,128)} %param.8) | copy-start | bytes 52
  8.2 28.2 %copy-start.1 = (f32[2,256,256]{2,1,0:T(8,128)S(1)}, f32[2,256,256]{2,1,0:T(8,128)}, u32[]{:S(2)}) copy-start(f32[2,256,256]{2,1,0:T(8,128)} %param.6) | copy-start | bytes 1572868
  8.2 15.7 %collective-permute-start = (f32[2,128,256]{2,1,0:T(8,128)S(1)}, f32[2,128,256]{2,1,0:T(8,128)S(1)}, u32[]{:S(2)}, u32[]{:S(2)}) collective-permute-start(f32[2,128,256]{2,1,0:T(8,128)S(1)} %slice.127), channel_id=1, source_target_pairs={{8,0},{16,8},{24,16},{32,24},{40,32},{48,40},{56,48},{64,56},{72,6... | collective-permute-start | bytes 786440 | tf_op jit(solution)/shard_map/ppermute | solution.py:17
  23.9 12.5 %collective-permute-start.1 = (f32[2,384,128]{2,1,0:T(8,128)S(1)}, f32[2,384,128]{2,1,0:T(8,128)S(1)}, u32[]{:S(2)}, u32[]{:S(2)}) collective-permute-start(f32[2,384,128]{2,1,0:T(8,128)S(1)} %slice.162), channel_id=1, source_target_pairs={{1,0},{2,1},{3,2},{4,3},{5,4},{6,5},{7,6},{9,8},{10,9},{11,10},{12... | collective-permute-start | bytes 1179656 | tf_op jit(solution)/shard_map/ppermute | solution.py:17
  45.5 1.7 copy-start
  75.4 7.5 %collective-permute-start.2 = (f32[2,384,128]{2,1,0:T(8,128)S(1)}, f32[2,384,128]{2,1,0:T(8,128)}, u32[]{:S(2)}, u32[]{:S(2)}) collective-permute-start(f32[2,384,128]{2,1,0:T(8,128)S(1)} %slice.170), channel_id=1, source_target_pairs={{0,1},{1,2},{2,3},{3,4},{4,5},{5,6},{6,7},{8,9},{9,10},{10,11},{11... | collective-permute-start | bytes 1179656 | tf_op jit(solution)/shard_map/ppermute | solution.py:17
  79.1 590.2 %all-reduce.5.cloned.1.call-start = ((), (), s32[]{:S(2)}) async-start(), calls=%async_computation.1 | async-start | bytes 1048576 | tf_op jit(solution)/shard_map/psum | solution.py:124
  84.0 271.8 %collective-permute-start.3 = (f32[2,128,256]{2,1,0:T(8,128)S(1)}, f32[2,128,256]{2,1,0:T(8,128)S(1)}, u32[]{:S(2)}, u32[]{:S(2)}) collective-permute-start(f32[2,128,256]{2,1,0:T(8,128)S(1)} %fusion.56), channel_id=1, source_target_pairs={{0,8},{8,16},{16,24},{24,32},{32,40},{40,48},{48,56},{56,64},{64,7... | collective-permute-start | bytes 786440 | tf_op jit(solution)/shard_map/ppermute | solution.py:17
  187.6 168.3 %copy-start.2 = (f32[2,256,256]{2,1,0:T(8,128)S(1)}, f32[2,256,256]{2,1,0:T(8,128)}, u32[]{:S(2)}) copy-start(f32[2,256,256]{2,1,0:T(8,128)} %param.5) | copy-start | bytes 1572868
  356.0 12.6 %copy-start.4 = (f32[2,256,256]{2,1,0:T(8,128)S(1)}, f32[2,256,256]{2,1,0:T(8,128)}, u32[]{:S(2)}) copy-start(f32[2,256,256]{2,1,0:T(8,128)} %all-reduce.3.cloned.1.call-done) | copy-start | bytes 1572868
  356.0 10.1 %collective-permute-start.4 = (f32[2,128,256]{2,1,0:T(8,128)S(1)}, f32[2,128,256]{2,1,0:T(8,128)S(1)}, u32[]{:S(2)}, u32[]{:S(2)}) collective-permute-start(f32[2,128,256]{2,1,0:T(8,128)S(1)} %slice.177), channel_id=1, source_target_pairs={{8,0},{16,8},{24,16},{32,24},{40,32},{48,40},{56,48},{64,56},{72,6... | collective-permute-start | bytes 786440 | tf_op jit(solution)/shard_map/ppermute | solution.py:17
  366.1 9.1 %collective-permute-start.5 = (f32[2,384,128]{2,1,0:T(8,128)S(1)}, f32[2,384,128]{2,1,0:T(8,128)S(1)}, u32[]{:S(2)}, u32[]{:S(2)}) collective-permute-start(f32[2,384,128]{2,1,0:T(8,128)S(1)} %pad_maximum_fusion.7), channel_id=1, source_target_pairs={{1,0},{2,1},{3,2},{4,3},{5,4},{6,5},{7,6},{9,8},{10,9},{11,10},{12... | collective-permute-start | bytes 1179656 | tf_op jit(solution)/shard_map/ppermute | solution.py:17
  413.1 260.0 %collective-permute-start.6 = (f32[2,384,128]{2,1,0:T(8,128)S(1)}, f32[2,384,128]{2,1,0:T(8,128)}, u32[]{:S(2)}, u32[]{:S(2)}) collective-permute-start(f32[2,384,128]{2,1,0:T(8,128)S(1)} %slice.186), channel_id=1, source_target_pairs={{0,1},{1,2},{2,3},{3,4},{4,5},{5,6},{6,7},{8,9},{9,10},{10,11},{11... | collective-permute-start | bytes 1179656 | tf_op jit(solution)/shard_map/ppermute | solution.py:17
  673.1 3.1 copy-start.3
  674.3 12.1 %collective-permute-start.7 = (f32[2,128,256]{2,1,0:T(8,128)S(1)}, f32[2,128,256]{2,1,0:T(8,128)S(1)}, u32[]{:S(2)}, u32[]{:S(2)}) collective-permute-start(f32[2,128,256]{2,1,0:T(8,128)S(1)} %fusion.53), channel_id=1, source_target_pairs={{0,8},{8,16},{16,24},{24,32},{32,40},{40,48},{48,56},{56,64},{64,7... | collective-permute-start | bytes 786440 | tf_op jit(solution)/shard_map/ppermute | solution.py:17
Sparse Core Ops, SparseCore 0:
  79.2 274.1 all-reduce.2
  398.1 271.1 all-reduce.4
where the time goes:
time: 704 us; the launch traced here: 694 us
  waiting for transfers between devices  351 us (50%)
  blocking collectives  199 us (28%)
  matrix products  42.7 us (6%)
  local copies, waits for them, and re-layouts  33.5 us (5%)
  between operations  28.6 us (4%)
  starting transfers between devices  27.3 us (4%)
  other arithmetic  11.8 us (2%)
    psum x2, waiting for transfers between devices, shards(): lax.psum((probe_grad, power_sum), ('row', 'col'))  321 us
    psum x2, blocking collectives, shards(): lax.psum((probe_grad, power_sum), ('row', 'col'))  199 us
    ppermute x8, waiting for transfers between devices, shifted(): return lax.ppermute(value, axis, pairs)  30.1 us
    dynamic_update_slice x4, local copies, waits for them, and re-layouts, add_window(): lax.dynamic_update_slice(grid_now, present + terms, (zero_index, first_ro...  29.2 us
    ppermute x8, starting transfers between devices, shifted(): return lax.ppermute(value, axis, pairs)  27.2 us
    dot_general x8, matrix products, complex_product(): jnp.einsum(pattern, real_part, matrices[1], precision=lax.Precision.HIGHEST)  15.1 us
  transfers between devices with their start and end apart: 10, of which 7 were waited for; matrix products, arithmetic and copies ran while one was open for 3% of the time, Pallas kernels for 0%

commit v1 on v0

--- a/solution.py
+++ b/solution.py
@@ -1,3 +1,4 @@
+import functools
 import math
 import jax
 import jax.numpy as jnp
@@ -9,6 +10,15 @@
 smooth_floor = 0.5
 object_step = 0.5
 tiny_value = 1e-06
+
+
+def fix_the_points(matrix, mesh_name, shard_axis):
+    for p in (mesh_name, shard_axis):
+        matrix = lax.psum(matrix, p)
+    return matrix
+
+
+get_ends = functools.partial(fix_the_points, mesh_name="col", shard_axis="row")
 
 
 def shifted(value, axis, by):
@@ -121,7 +131,7 @@
         )
         current = current + object_step * tile_grad / (probe_mean + tiny_value)
         power_old = jnp.sum(probe_now * probe_now)
-        summed_grad, summed_power = lax.psum((probe_grad, power_sum), ("row", "col"))
+        summed_grad, summed_power = get_ends((probe_grad, power_sum))
         moved_probe = probe_now + summed_grad / (summed_power / (window * window) + tiny_value)
         power_new = jnp.sum(moved_probe * moved_probe)
         probe_now = moved_probe * jnp.sqrt(power_old / (power_new + tiny_value))

time: 704 us -> 624 us (0.89)
  the two profiles are of different devices: /device:TPU:21 before, /device:TPU:32 now
where the time goes in v1:
time: 624 us; the launch traced here: 614 us
  blocking collectives  312 us (50%)
  waiting for transfers between devices  153 us (25%)
  matrix products  43 us (7%)
  local copies, waits for them, and re-layouts  34 us (5%)
  starting transfers between devices  32.2 us (5%)
  between operations  28.4 us (5%)
  other arithmetic  11.7 us (2%)
    psum x4, blocking collectives, fix_the_points(): matrix = lax.psum(matrix, p)  312 us
    psum x4, waiting for transfers between devices, fix_the_points(): matrix = lax.psum(matrix, p)  142 us
    ppermute x8, starting transfers between devices, shifted(): return lax.ppermute(value, axis, pairs)  32 us
    dynamic_update_slice x4, local copies, waits for them, and re-layouts, add_window(): lax.dynamic_update_slice(grid_now, present + terms, (zero_index, first_ro...  29.7 us
    dot_general x8, matrix products, complex_product(): jnp.einsum(pattern, real_part, matrices[1], precision=lax.Precision.HIGHEST)  15.4 us
    dot_general x8, matrix products, complex_product(): jnp.einsum(pattern, real_part + imag_part, matrices[0], precision=lax.Pre...  13.8 us
    dot_general x8, matrix products, complex_product(): jnp.einsum(pattern, imag_part, matrices[2], precision=lax.Precision.HIGHEST)  13.8 us
  transfers between devices with their start and end apart: 12, of which 5 were waited for; matrix products, arithmetic and copies ran while one was open for 1% of the time, Pallas kernels for 0%

profile of v1, /device:TPU:32, one launch (start us, length us, event | category | flops | bytes accessed | tf_op | source)
XLA Modules:
  0.0 614.2 jit_solution(5505567327364875622)
XLA Ops:
  8.2 11.0 %collective-permute-start = (f32[2,128,256]{2,1,0:T(8,128)S(1)}, f32[2,128,256]{2,1,0:T(8,128)S(1)}, u32[]{:S(2)}, u32[]{:S(2)}) collective-permute-start(f32[2,128,256]{2,1,0:T(8,128)S(1)} %slice.127), channel_id=1, source_target_pairs={{8,0},{16,8},{24,16},{32,24},{40,32},{48,40},{56,48},{64,56},{72,6... | collective-permute-start | bytes 786440 | tf_op jit(solution)/shard_map/ppermute | solution.py:27
  20.3 4.5 collective-permute-done
  24.8 1.3 collective-permute-start.1
  35.9 1.6 fusion.48
  37.5 1.7 convolution_add_fusion.7
  39.2 1.7 convolution_subtract_fusion.7
  40.9 1.7 fusion.46
  42.5 1.7 fusion.10
  44.3 1.7 fusion.11
  46.0 2.0 fusion.42
  48.1 1.8 convolution_add_fusion.5
  49.8 1.8 convolution_subtract_fusion.5
  51.6 1.7 fusion.40
  53.2 1.7 fusion.9
  55.0 2.4 add_reduce_fusion.1
  58.3 7.4 %dynamic_update_slice.12 = f32[2,384,384]{2,1,0:T(8,128)S(1)} dynamic-update-slice(f32[2,384,384]{2,1,0:T(8,128)S(1)} %broadcast.28.clone, f32[2,256,256]{2,1,0:T(8,128)S(1)} %pad_maximum_fusion.3, s32[]{:T(128)} %constant.29.clone.1, s32[]{:T(128)S(6)} %select_n.82, s32[]{:T(128)S(6)} %select_n.83) | dynamic-update-slice | bytes 1048580 | tf_op jit(solution)/shard_map/dynamic_update_slice | solution.py:67
  65.7 1.2 maximum_add_fusion
  66.9 7.4 %dynamic_update_slice.13 = f32[2,384,384]{2,1,0:T(8,128)S(1)} dynamic-update-slice(f32[2,384,384]{2,1,0:T(8,128)S(1)} %dynamic_update_slice.12, f32[2,256,256]{2,1,0:T(8,128)S(1)} %maximum_add_fusion, s32[]{:T(128)} %constant.29.clone.1, s32[]{:T(128)S(6)} %select_n.84, s32[]{:T(128)S(6)} %select_n.85) | dynamic-update-slice | bytes 1048580 | tf_op jit(solution)/shard_map/dynamic_update_slice | solution.py:67
  74.3 3.6 collective-permute-start.2
  78.9 71.8 %all-reduce.5.cloned.1.call-done = f32[2,256,256]{2,1,0:T(8,128)} async-done(((f32[2,256,256]{2,1,0:T(8,128)}), f32[2,256,256]{2,1,0:T(8,128)}) %all-reduce.5.cloned.1.call-update) | async-done | bytes 524304 | tf_op jit(solution)/shard_map/psum | solution.py:17
  151.8 3.6 collective-permute-start.3
  155.4 13.9 %psum.58 = f32[]{:T(128)} all-reduce(f32[]{:T(128)} %get-tuple-element.7), channel_id=1, replica_groups=mesh['row'=64,'col'=8] {'col'}, use_global_device_ids=true, to_apply=%region_6.7 | all-reduce | flops 1 | bytes 8 | tf_op jit(solution)/shard_map/psum | solution.py:17
  169.3 142.1 %psum.59 = f32[]{:T(128)} all-reduce(f32[]{:T(128)} %psum.58), channel_id=1, replica_groups=mesh['row'=64,'col'=8] {'row'}, use_global_device_ids=true, to_apply=%region_7.8 | all-reduce | flops 1 | bytes 8 | tf_op jit(solution)/shard_map/psum | solution.py:17
  312.1 1.8 multiply_reduce_fusion.3
  314.7 2.1 collective-permute-start.4
  318.2 4.9 collective-permute-done.4
  323.1 1.5 collective-permute-start.5
  324.8 2.0 collective-permute-done.5
  327.3 1.6 fusion.38
  328.9 1.7 convolution_add_fusion.3
  330.6 1.7 convolution_subtract_fusion.3
  332.3 1.7 fusion.36
  334.0 1.7 fusion.4
  335.7 1.7 fusion.5
  337.4 1.9 fusion.32
  339.3 1.7 convolution_add_fusion.1
  341.1 1.8 convolution_subtract_fusion.1
  342.9 1.7 fusion.30
  344.5 1.7 fusion.3
  346.3 2.7 add_reduce_fusion
  349.2 7.4 %dynamic_update_slice.14 = f32[2,384,384]{2,1,0:T(8,128)S(1)} dynamic-update-slice(f32[2,384,384]{2,1,0:T(8,128)S(1)} %broadcast.28, f32[2,256,256]{2,1,0:T(8,128)S(1)} %pad_maximum_fusion.5, s32[]{:T(128)} %constant.29.clone.1, s32[]{:T(128)S(6)} %select_n.82, s32[]{:T(128)S(6)} %select_n.83) | dynamic-update-slice | bytes 1048580 | tf_op jit(solution)/shard_map/dynamic_update_slice | solution.py:67
  356.8 7.4 %dynamic_update_slice.15 = f32[2,384,384]{2,1,0:T(8,128)S(1)} dynamic-update-slice(f32[2,384,384]{2,1,0:T(8,128)S(1)} %dynamic_update_slice.14, f32[2,256,256]{2,1,0:T(8,128)S(1)} %maximum_add_fusion.1, s32[]{:T(128)} %constant.29.clone.1, s32[]{:T(128)S(6)} %select_n.84, s32[]{:T(128)S(6)} %select_n.85) | dynamic-update-slice | bytes 1048580 | tf_op jit(solution)/shard_map/dynamic_update_slice | solution.py:67
  364.3 5.4 collective-permute-start.6
  370.6 69.7 %all-reduce.9.cloned.1.call-done = f32[2,256,256]{2,1,0:T(8,128)} async-done(((f32[2,256,256]{2,1,0:T(8,128)}), f32[2,256,256]{2,1,0:T(8,128)}) %all-reduce.9.cloned.1.call-update) | async-done | bytes 524304 | tf_op jit(solution)/shard_map/psum | solution.py:17
  441.5 3.6 collective-permute-start.7
  445.0 13.9 %psum.62 = f32[]{:T(128)} all-reduce(f32[]{:T(128)} %get-tuple-element.6), channel_id=1, replica_groups=mesh['row'=64,'col'=8] {'col'}, use_global_device_ids=true, to_apply=%region_15.16 | all-reduce | flops 1 | bytes 8 | tf_op jit(solution)/shard_map/psum | solution.py:17
  459.0 142.0 %psum.63 = f32[]{:T(128)} all-reduce(f32[]{:T(128)} %psum.62), channel_id=1, replica_groups=mesh['row'=64,'col'=8] {'row'}, use_global_device_ids=true, to_apply=%region_16.17 | all-reduce | flops 1 | bytes 8 | tf_op jit(solution)/shard_map/psum | solution.py:17
  601.7 1.8 multiply_reduce_fusion
  (66 shorter events, 11.5 us)
Async XLA Ops:
  7.2 143.5 %all-reduce.5.cloned.1.call-start = ((), (), s32[]{:S(2)}) async-start(), calls=%async_computation | async-start | bytes 1048576 | tf_op jit(solution)/shard_map/psum | solution.py:17
  8.2 17.9 %copy-start.6 = (s32[1,1,2,2]{3,2,1,0:T(2,128)S(1)}, s32[1,1,2,2]{3,2,1,0:T(2,128)}, u32[]{:S(2)}) copy-start(s32[1,1,2,2]{3,2,1,0:T(2,128)} %param.8) | copy-start | bytes 52
  8.2 26.9 %copy-start.1 = (f32[2,256,256]{2,1,0:T(8,128)S(1)}, f32[2,256,256]{2,1,0:T(8,128)}, u32[]{:S(2)}) copy-start(f32[2,256,256]{2,1,0:T(8,128)} %param.6) | copy-start | bytes 1572868
  8.2 16.5 %collective-permute-start = (f32[2,128,256]{2,1,0:T(8,128)S(1)}, f32[2,128,256]{2,1,0:T(8,128)S(1)}, u32[]{:S(2)}, u32[]{:S(2)}) collective-permute-start(f32[2,128,256]{2,1,0:T(8,128)S(1)} %slice.127), channel_id=1, source_target_pairs={{8,0},{16,8},{24,16},{32,24},{40,32},{48,40},{56,48},{64,56},{72,6... | collective-permute-start | bytes 786440 | tf_op jit(solution)/shard_map/ppermute | solution.py:27
  24.8 10.3 %collective-permute-start.1 = (f32[2,384,128]{2,1,0:T(8,128)S(1)}, f32[2,384,128]{2,1,0:T(8,128)S(1)}, u32[]{:S(2)}, u32[]{:S(2)}) collective-permute-start(f32[2,384,128]{2,1,0:T(8,128)S(1)} %slice.162), channel_id=1, source_target_pairs={{1,0},{2,1},{3,2},{4,3},{5,4},{6,5},{7,6},{9,8},{10,9},{11,10},{12... | collective-permute-start | bytes 1179656 | tf_op jit(solution)/shard_map/ppermute | solution.py:27
  44.3 1.7 copy-start
  74.3 76.4 %collective-permute-start.2 = (f32[2,384,128]{2,1,0:T(8,128)S(1)}, f32[2,384,128]{2,1,0:T(8,128)}, u32[]{:S(2)}, u32[]{:S(2)}) collective-permute-start(f32[2,384,128]{2,1,0:T(8,128)S(1)} %slice.170), channel_id=1, source_target_pairs={{0,1},{1,2},{2,3},{3,4},{4,5},{5,6},{6,7},{8,9},{9,10},{10,11},{11... | collective-permute-start | bytes 1179656 | tf_op jit(solution)/shard_map/ppermute | solution.py:27
  78.8 233.3 %all-reduce.7.cloned.1.call-start = ((), (), s32[]{:S(2)}) async-start(), calls=%async_computation.1 | async-start | bytes 1048576 | tf_op jit(solution)/shard_map/psum | solution.py:17
  150.7 289.7 %all-reduce.9.cloned.1.call-start = ((), (), s32[]{:S(2)}) async-start(), calls=%async_computation.2 | async-start | bytes 1048576 | tf_op jit(solution)/shard_map/psum | solution.py:17
  151.8 160.2 %collective-permute-start.3 = (f32[2,128,256]{2,1,0:T(8,128)S(1)}, f32[2,128,256]{2,1,0:T(8,128)S(1)}, u32[]{:S(2)}, u32[]{:S(2)}) collective-permute-start(f32[2,128,256]{2,1,0:T(8,128)S(1)} %fusion.56), channel_id=1, source_target_pairs={{0,8},{8,16},{16,24},{24,32},{32,40},{40,48},{48,56},{56,64},{64,7... | collective-permute-start | bytes 786440 | tf_op jit(solution)/shard_map/ppermute | solution.py:27
  312.0 2.6 copy-start.2
  314.7 9.9 %copy-start.3 = (f32[2,256,256]{2,1,0:T(8,128)S(1)}, f32[2,256,256]{2,1,0:T(8,128)}, u32[]{:S(2)}) copy-start(f32[2,256,256]{2,1,0:T(8,128)} %all-reduce.7.cloned.1.call-done) | copy-start | bytes 1572868
  314.7 8.4 %collective-permute-start.4 = (f32[2,128,256]{2,1,0:T(8,128)S(1)}, f32[2,128,256]{2,1,0:T(8,128)S(1)}, u32[]{:S(2)}, u32[]{:S(2)}) collective-permute-start(f32[2,128,256]{2,1,0:T(8,128)S(1)} %slice.177), channel_id=1, source_target_pairs={{8,0},{16,8},{24,16},{32,24},{40,32},{48,40},{56,48},{64,56},{72,6... | collective-permute-start | bytes 786440 | tf_op jit(solution)/shard_map/ppermute | solution.py:27
  323.1 3.6 collective-permute-start.5
  356.8 12.9 %copy-start.5 = (f32[256,256]{1,0:T(8,128)S(1)}, f32[256,256]{1,0:T(8,128)}, u32[]{:S(2)}) copy-start(f32[256,256]{1,0:T(8,128)} %get-tuple-element.3) | copy-start | bytes 786436
  364.3 76.1 %collective-permute-start.6 = (f32[2,384,128]{2,1,0:T(8,128)S(1)}, f32[2,384,128]{2,1,0:T(8,128)}, u32[]{:S(2)}, u32[]{:S(2)}) collective-permute-start(f32[2,384,128]{2,1,0:T(8,128)S(1)} %slice.186), channel_id=1, source_target_pairs={{0,1},{1,2},{2,3},{3,4},{4,5},{5,6},{6,7},{8,9},{9,10},{10,11},{11... | collective-permute-start | bytes 1179656 | tf_op jit(solution)/shard_map/ppermute | solution.py:27
  370.5 231.2 %all-reduce.11.cloned.1.call-start = ((), (), s32[]{:S(2)}) async-start(), calls=%async_computation.3 | async-start | bytes 1048576 | tf_op jit(solution)/shard_map/psum | solution.py:17
  441.5 160.2 %collective-permute-start.7 = (f32[2,128,256]{2,1,0:T(8,128)S(1)}, f32[2,128,256]{2,1,0:T(8,128)S(1)}, u32[]{:S(2)}, u32[]{:S(2)}) collective-permute-start(f32[2,128,256]{2,1,0:T(8,128)S(1)} %fusion.53), channel_id=1, source_target_pairs={{0,8},{8,16},{16,24},{24,32},{32,40},{40,48},{48,56},{56,64},{64,7... | collective-permute-start | bytes 786440 | tf_op jit(solution)/shard_map/ppermute | solution.py:27
  603.5 2.9 copy-start.4
Sparse Core Ops, SparseCore 0:
  78.9 71.6 all-reduce.4
  153.9 155.0 all-reduce.6
  370.7 69.6 all-reduce.8
  443.4 154.9 all-reduce.10
